TPU v7x, 32 devices: a whole 2x2x4 slice. The times are simulated.
32 devices in a mesh: dp: 4 (over y, x), section: 2 (over core), tensor: 4 (over z).
Axes of the slice: x: 2, y: 2, z: 4, core: 2. Of those that a mesh axis runs over, the one named last changes fastest.
Arguments:
- in_delta: bfloat16 [8, 1024, 4096], P(None, ('dp', 'tensor')), may hold values from -12 to 12
- weight: bfloat16 [2, 4096, 4096], P('section', 'tensor'), may hold values from -0.09375 to 0.09375
- cache_codes: int32 [2, 2, 8, 1024, 4096], P('section', None, None, ('dp', 'tensor')), may hold values from -7 to 7, as said below
- cache_scales: float32 [2, 2, 8, 4, 32], P('section', None, None, 'dp'), may hold values from 0.2 to 6, as said below
- cotangent: bfloat16 [8, 1024, 4096], P(None, ('dp', 'tensor')), may hold values from -6 to 6
Outputs:
- out_deltas: bfloat16 [2, 8, 1024, 4096], P('section', None, ('dp', 'tensor'))
- grad_in: bfloat16 [2, 8, 1024, 4096], P('section', None, ('dp', 'tensor'))
- weight_grad: float32 [2, 4096, 4096], P('section', 'tensor', 'dp')
Inputs may be any that keep to these rules, and one draw needn't show every extreme that they name: cache_codes[s, 1] equals cache_codes[s + 1, 0]: the buffer of a boundary between two segments is held by both. cache_scales[s, 1] equals cache_scales[s + 1, 0].
All inputs are finite; a program needn't handle non-finite values. Where the computation divides by a largest or mean magnitude, that divisor is 1e-20 or more.
Results may differ from a plain program's by a relative error of at most 0.013.
Values may be sent and summed in bfloat16 or wider, within the bound.
A program may use at most 320 MiB of HBM per device.

v0:
```python
import jax
import jax.numpy as jnp
from jax import lax
from jax.sharding import PartitionSpec as P

code_levels = 7.0
softness = 0.8
two_pi = 6.283185307179586
epsilon = 1e-06
bf16 = jnp.bfloat16
f32 = jnp.float32
chunk_count = 1
sine_terms = (
    6.283185307179586,
    -41.34170224039975,
    81.60524927607504,
    -76.70585975306136,
    42.058693944897655,
    -15.094642576822984,
    3.819952584848282,
)


def sine_of_turns(turns):
    rest = turns - jnp.round(turns)
    rest = jnp.where(rest > 0.25, 0.5 - rest, jnp.where(rest < -0.25, -0.5 - rest, rest))
    square = rest * rest
    total = jnp.full_like(rest, sine_terms[-1])
    for term in sine_terms[-2::-1]:
        total = total * square + term
    return total * rest


def local(in_delta, weight, cache_codes, cache_scales, cotangent):
    dp_count = lax.axis_size("dp")
    section_count = lax.axis_size("section")
    replica = lax.axis_index("dp")
    first = lax.axis_index("section") == 0
    micro_count, rows, width = in_delta.shape
    block_count = cache_scales.shape[-1]
    block = width // block_count
    part = width // dp_count
    is_power = dp_count & dp_count - 1 == 0
    chunks = chunk_count if micro_count % chunk_count == 0 else 1
    micros = micro_count // chunks
    tokens = micros * rows

    def target(source, step):
        return source ^ step if is_power else (source + step) % dp_count

    def origin(source, step):
        return source ^ step if is_power else (source - step) % dp_count

    def exchange(value, section, step):
        pairs = [
            (source * section_count + section, target(source, step) * section_count + section)
            for source in range(dp_count)
        ]
        return lax.ppermute(value, ("dp", "section"), pairs)

    def give_back(value, section, step):
        pairs = [
            (source * section_count + section, origin(source, step) * section_count + section)
            for source in range(dp_count)
        ]
        return lax.ppermute(value, ("dp", "section"), pairs)

    def columns(value, index):
        return lax.dynamic_slice_in_dim(value, index * part, part, 1)

    weight_part = lax.all_gather(columns(weight[0], replica), "tensor", axis=0, tiled=True)

    def product(forward_here, whole, piece):

        def forward(whole, piece):
            out = jnp.dot(whole, weight_part, preferred_element_type=f32).astype(bf16)
            return (out, jnp.zeros((tokens, width), bf16))

        def backward(whole, piece):
            out = lax.dot_general(
                piece, weight_part, (((1,), (1,)), ((), ())), preferred_element_type=f32
            ).astype(bf16)
            return (jnp.zeros((tokens, part), bf16), out)

        return lax.cond(forward_here, forward, backward, whole, piece)

    def pre(normed, upstream, forward_section):
        whole, piece = ([normed], [columns(upstream, replica)])
        for step in range(1, dp_count):
            whole.append(exchange(normed, forward_section, step))
            piece.append(
                exchange(columns(upstream, target(replica, step)), 1 - forward_section, step)
            )
        return (whole, piece)

    def middle(whole, piece, forward_section):
        here = first if forward_section == 0 else ~first
        branch = jnp.zeros((tokens, width), bf16)
        grad = None
        order = list(range(1, dp_count)) + [0]
        for step in order:
            out, back = product(here, whole[step], piece[step])
            if step:
                out = give_back(out, forward_section, step)
                back = give_back(back, 1 - forward_section, step)
            branch = lax.dynamic_update_slice_in_dim(branch, out, target(replica, step) * part, 1)
            grad = back.astype(f32) if grad is None else grad + back.astype(f32)
        return (branch, grad)

    def scales_row(slot, chunk):
        now = cache_scales[0, slot, chunk * micros : (chunk + 1) * micros, 0]
        return jnp.repeat(now / code_levels, block, axis=-1)[:, None, :]

    def codes(slot, chunk):
        return cache_codes[0, slot, chunk * micros : (chunk + 1) * micros].astype(f32)

    def shaped(value):
        return value.reshape(micros, rows, width)

    def flat(value):
        return value.reshape(tokens, width)

    def rms(hidden):
        return lax.rsqrt(jnp.mean(hidden * hidden, axis=-1, keepdims=True) + epsilon)

    def finish_forward(hidden, branch, chunk):
        delta = hidden + shaped(branch).astype(f32) - codes(1, chunk) * scales_row(1, chunk)
        peak = jnp.max(jnp.abs(delta), axis=1).reshape(micros, block_count, block).max(axis=-1)
        spread = lax.pmax(peak, "tensor") + epsilon
        up_scale = jnp.repeat(code_levels / spread, block, axis=-1)[:, None, :]
        down_scale = jnp.repeat(spread / code_levels, block, axis=-1)[:, None, :]
        level = delta * up_scale
        smooth = level - softness / two_pi * sine_of_turns(level)
        return (smooth * down_scale).astype(bf16)

    def finish_backward(hidden, upstream, grad):
        inverse = rms(hidden)
        grad = shaped(grad.astype(bf16)).astype(f32)
        unrounded = hidden * inverse
        mean = jnp.mean(grad * unrounded, axis=-1, keepdims=True)
        return (upstream.astype(f32) + inverse * (grad - unrounded * mean)).astype(bf16)

    over = range(chunks)
    span = [slice(c * micros, (c + 1) * micros) for c in over]
    outs, grads, wholes, pieces = ([None] * chunks, [None] * chunks, [], [])
    with jax.named_scope("phase_a"):
        stage_a = []
        for c in over:
            hidden = codes(0, c) * scales_row(0, c) + in_delta[span[c]].astype(f32)
            normed = flat((hidden * rms(hidden)).astype(bf16))
            stage_a.append((hidden, pre(normed, flat(cotangent[span[c]]), 0)))
        stage_b = []
        for c in over:
            hidden, (whole, piece) = stage_a[c]
            branch, grad = middle(whole, piece, 0)
            outs[c] = finish_forward(hidden, branch, c)
            received = lax.ppermute(outs[c], "section", [(0, 1)])
            incoming = jnp.where(first, in_delta[span[c]], received)
            hidden = codes(0, c) * scales_row(0, c) + incoming.astype(f32)
            normed = flat((hidden * rms(hidden)).astype(bf16))
            grads[c] = finish_backward(hidden, cotangent[span[c]], grad)
            upstream = lax.ppermute(grads[c], "section", [(1, 0)])
            stage_b.append((hidden, upstream, pre(normed, flat(upstream), 1)))
    with jax.named_scope("weight_grad"):

        def gathered(pairs):
            whole = jnp.concatenate([w for p in pairs for w in p[0]], axis=0)
            piece = jnp.concatenate([g for p in pairs for g in p[1]], axis=0)
            return lax.dot_general(
                whole, piece, (((0,), (0,)), ((), ())), preferred_element_type=f32
            ).astype(bf16)

        from_a = [a[1] for a in stage_a]
        from_b = [b[2] for b in stage_b]
        partial = lax.cond(
            first,
            lambda a, b: gathered([(x[0], y[1]) for x, y in zip(a, b)]),
            lambda a, b: gathered([(y[0], x[1]) for x, y in zip(a, b)]),
            from_a,
            from_b,
        )
        weight_grad = lax.psum_scatter(partial, "tensor", scatter_dimension=0, tiled=True).astype(
            f32
        )
    with jax.named_scope("phase_b"):
        for c in over:
            hidden, upstream, (whole, piece) = stage_b[c]
            branch, grad = middle(whole, piece, 1)
            outs[c] = jnp.where(first, outs[c], finish_forward(hidden, branch, c))
            grads[c] = jnp.where(first, finish_backward(hidden, upstream, grad), grads[c])

    def joined(values):
        return values[0] if chunks == 1 else jnp.concatenate(values, axis=0)

    return (joined(outs)[None], joined(grads)[None], weight_grad[None])


def solution(mesh):
    return jax.shard_map(
        local,
        mesh=mesh,
        in_specs=(
            P(None, ("dp", "tensor"), None),
            P("section", "tensor", None),
            P("section", None, None, ("dp", "tensor"), None),
            P("section", None, None, "dp", None),
            P(None, ("dp", "tensor"), None),
        ),
        out_specs=(
            P("section", None, ("dp", "tensor"), None),
            P("section", None, ("dp", "tensor"), None),
            P("section", "tensor", "dp"),
        ),
        check_vma=False,
    )
```

profile of v0, /device:TPU:0, one launch (start us, length us, event | category | flops | bytes accessed | tf_op | source)
XLA Modules:
  0.0 650.8 jit_solution(17518955438547281373)
XLA Ops:
  42.7 120.1 %all-gather.3.cloned.1.call-done = bf16[1,4096,1024]{2,1,0:T(8,128)(2,1)} async-done(((bf16[1,1024,1024]{2,1,0:T(8,128)(2,1)}), bf16[1,4096,1024]{2,1,0:T(8,128)(2,1)}) %all-gather.3.cloned.1.call-update) | async-done | bytes 8388624 | tf_op jit(solution)/shard_map/all_gather | solution.py:71
  162.8 10.8 %conditional.13 = (bf16[512,1024]{1,0:T(8,128)(2,1)}, bf16[512,4096]{1,0:T(8,128)(2,1)S(1)}) conditional(s32[]{:T(128)} %convert_element_type.174, (bf16[512,1024]{1,0:T(8,128)(2,1)}, bf16[4096,1024]{1,0:T(8,128)(2,1)}) %tuple.157, (bf16[512,4096]{1,0:T(8,128)(2,1)}, bf16[4096,1024]{1,0:T(8,128)(2,1)}) %tuple.142), branch_computations={%region_1.0_spmd, %region_2.0_spmd} | conditional | flops 4297064448 | bytes 17825810 | solution.py:85
  162.8 10.3 %convolution_convert_fusion.1 = bf16[512,1024]{1,0:T(8,128)(2,1)} fusion(bf16[512,4096]{1,0:T(8,128)(2,1)} %get-tuple-element.105, bf16[4096,1024]{1,0:T(8,128)(2,1)} %get-tuple-element.106), kind=kOutput, calls=%fused_computation.1 | convolution fusion | flops 4295491584 | bytes 13631488 | tf_op jit(solution)/shard_map/phase_a/cond/branch_1_fun/dot_general | solution.py:76
  177.1 10.9 %conditional.14 = (bf16[512,1024]{1,0:T(8,128)(2,1)}, bf16[512,4096]{1,0:T(8,128)(2,1)S(1)}) conditional(s32[]{:T(128)} %convert_element_type.174, (bf16[512,1024]{1,0:T(8,128)(2,1)}, bf16[4096,1024]{1,0:T(8,128)(2,1)}) %tuple.143, (bf16[512,4096]{1,0:T(8,128)(2,1)}, bf16[4096,1024]{1,0:T(8,128)(2,1)}) %tuple.144), branch_computations={%region_3.0_spmd, %region_4.0_spmd} | conditional | flops 4297064448 | bytes 17825810 | solution.py:85
  191.4 11.1 %conditional.15 = (bf16[512,1024]{1,0:T(8,128)(2,1)}, bf16[512,4096]{1,0:T(8,128)(2,1)S(1)}) conditional(s32[]{:T(128)} %convert_element_type.174, (bf16[512,1024]{1,0:T(8,128)(2,1)}, bf16[4096,1024]{1,0:T(8,128)(2,1)}) %tuple.145, (bf16[512,4096]{1,0:T(8,128)(2,1)}, bf16[4096,1024]{1,0:T(8,128)(2,1)}) %tuple.146), branch_computations={%region_5.0_spmd, %region_6.0_spmd} | conditional | flops 4297064448 | bytes 17825810 | solution.py:85
  210.4 13.5 %conditional.16 = (bf16[512,1024]{1,0:T(8,128)(2,1)S(1)}, f32[512,4096]{1,0:T(8,128)}) conditional(s32[]{:T(128)} %convert_element_type.174, (bf16[512,1024]{1,0:T(8,128)(2,1)S(1)}, bf16[4096,1024]{1,0:T(8,128)(2,1)}) %tuple.147, (bf16[512,4096]{1,0:T(8,128)(2,1)}, bf16[4096,1024]{1,0:T(8,128)(2,1)}) %tuple.148), branch_computations={%region_7.0_spmd, %region_8.0_spmd} | conditional | flops 4299161600 | bytes 22020116 | solution.py:85
  243.1 15.9 %pmax.14 = f32[8,32]{0,1:T(8,128)S(1)} all-reduce(f32[8,32]{0,1:T(8,128)S(1)} %bitcast_reduce_fusion.1), channel_id=1, replica_groups=mesh['dp'=4,'section'=2,'tensor'=4] {'tensor'}, use_global_device_ids=true, to_apply=%region_11.0 | all-reduce | flops 256 | bytes 2048 | tf_op jit(solution)/shard_map/phase_a/pmax | solution.py:129
  271.6 10.5 %add_convert_fusion.1 = bf16[512,4096]{1,0:T(8,128)(2,1)} fusion(f32[512,4096]{1,0:T(8,128)} %get-tuple-element.177, bf16[512,4096]{1,0:T(8,128)(2,1)} %collective-permute-done.12, bf16[512,4096]{1,0:T(8,128)(2,1)} %collective-permute-done.11, bf16[512,4096]{1,0:T(8,128)(2,1)} %collective-permute-done.10), kind=kLoop, calls=%fused_computation.86 | loop fusion | flops 14680064 | bytes 25165824 | tf_op jit(solution)/shard_map/phase_a/convert_element_type | solution.py:138
  310.7 34.6 %collective-permute-done.13 = bf16[8,64,4096]{2,1,0:T(8,128)(2,1)S(1)} collective-permute-done((bf16[8,64,4096]{2,1,0:T(8,128)(2,1)S(1)}, bf16[8,64,4096]{2,1,0:T(8,128)(2,1)S(1)}, u32[]{:S(2)}, u32[]{:S(2)}) %collective-permute-start.13) | collective-permute-done | bytes 4194336 | tf_op jit(solution)/shard_map/phase_a/ppermute | solution.py:162
  357.1 18.8 %collective-permute-done.14 = bf16[512,1024]{1,0:T(8,128)(2,1)} collective-permute-done((bf16[512,1024]{1,0:T(8,128)(2,1)S(1)}, bf16[512,1024]{1,0:T(8,128)(2,1)}, u32[]{:S(2)}, u32[]{:S(2)}) %collective-permute-start.14) | collective-permute-done | bytes 1048608 | tf_op jit(solution)/shard_map/phase_a/ppermute | solution.py:59
  379.9 19.3 %collective-permute-done.20 = bf16[512,1024]{1,0:T(8,128)(2,1)} collective-permute-done((bf16[512,1024]{1,0:T(8,128)(2,1)S(1)}, bf16[512,1024]{1,0:T(8,128)(2,1)}, u32[]{:S(2)}, u32[]{:S(2)}) %collective-permute-start.20) | collective-permute-done | bytes 1048608 | tf_op jit(solution)/shard_map/phase_a/ppermute | solution.py:59
  399.3 24.0 %conditional.21 = (bf16[4096,1024]{1,0:T(8,128)(2,1)}) conditional(s32[]{:T(128)} %convert_element_type.174, (bf16[512,4096]{1,0:T(8,128)(2,1)}, bf16[512,4096]{1,0:T(8,128)(2,1)}, bf16[512,4096]{1,0:T(8,128)(2,1)}, bf16[512,4096]{1,0:T(8,128)(2,1)}, bf16[512,1024]{1,0:T(8,128)(2,1)S(1)}, /*index=5*/bf16[512,1024]{1,0:T(8,128)(2,1)}, ...), branch_computations={%region_26.27_spmd, %region_27.28_spmd} | conditional | flops 17263755264 | bytes 29360136
  399.5 23.8 %fusion.18 = bf16[4096,1024]{1,0:T(8,128)(2,1)} fusion(bf16[512,4096]{1,0:T(8,128)(2,1)} %get-tuple-element.146, bf16[512,4096]{1,0:T(8,128)(2,1)} %get-tuple-element.145, bf16[512,4096]{1,0:T(8,128)(2,1)} %get-tuple-element.144, bf16[512,4096]{1,0:T(8,128)(2,1)} %get-tuple-element.143, bf16[512,1024]{1,0:T(8,128)(2,1)} %get-tuple-element.150, ...), kind=kOutput, calls=%fused_computation.34 | convolution fusion | flops 17263755264 | bytes 29360128 | tf_op jit(solution)/shard_map/weight_grad/cond/branch_1_fun/dot_general | solution.py:169
  423.3 10.8 %conditional.17 = (bf16[512,1024]{1,0:T(8,128)(2,1)S(1)}, bf16[512,4096]{1,0:T(8,128)(2,1)}) conditional(s32[]{:T(128)} %convert_element_type.182, (bf16[512,1024]{1,0:T(8,128)(2,1)}, bf16[4096,1024]{1,0:T(8,128)(2,1)}) %tuple.149, (bf16[512,4096]{1,0:T(8,128)(2,1)}, bf16[4096,1024]{1,0:T(8,128)(2,1)}) %tuple.150), branch_computations={%region_14.15_spmd, %region_15.16_spmd} | conditional | flops 4297064448 | bytes 17825810 | solution.py:85
  436.6 10.6 %conditional.18 = (bf16[512,1024]{1,0:T(8,128)(2,1)S(1)}, bf16[512,4096]{1,0:T(8,128)(2,1)}) conditional(s32[]{:T(128)} %convert_element_type.182, (bf16[512,1024]{1,0:T(8,128)(2,1)}, bf16[4096,1024]{1,0:T(8,128)(2,1)}) %tuple.151, (bf16[512,4096]{1,0:T(8,128)(2,1)}, bf16[4096,1024]{1,0:T(8,128)(2,1)}) %tuple.152), branch_computations={%region_16.17_spmd, %region_17.18_spmd} | conditional | flops 4297064448 | bytes 17825810 | solution.py:85
  436.6 10.3 %convolution_convert_fusion.10 = bf16[512,4096]{1,0:T(8,128)(2,1)} fusion(bf16[512,1024]{1,0:T(8,128)(2,1)} %get-tuple-element.123, bf16[4096,1024]{1,0:T(8,128)(2,1)} %get-tuple-element.124), kind=kOutput, calls=%fused_computation.11 | convolution fusion | flops 4297064448 | bytes 13631488 | tf_op jit(solution)/shard_map/phase_b/cond/branch_0_fun/dot_general | solution.py:80
  449.7 11.4 %conditional.19 = (bf16[512,1024]{1,0:T(8,128)(2,1)}, bf16[512,4096]{1,0:T(8,128)(2,1)}) conditional(s32[]{:T(128)} %convert_element_type.182, (bf16[512,1024]{1,0:T(8,128)(2,1)}, bf16[4096,1024]{1,0:T(8,128)(2,1)}) %tuple.153, (bf16[512,4096]{1,0:T(8,128)(2,1)}, bf16[4096,1024]{1,0:T(8,128)(2,1)}) %tuple.154), branch_computations={%region_18.19_spmd, %region_19.20_spmd} | conditional | flops 4297064448 | bytes 17825810 | solution.py:85
  449.7 10.3 %convolution_convert_fusion.12 = bf16[512,4096]{1,0:T(8,128)(2,1)} fusion(bf16[512,1024]{1,0:T(8,128)(2,1)} %get-tuple-element.127, bf16[4096,1024]{1,0:T(8,128)(2,1)} %get-tuple-element.128), kind=kOutput, calls=%fused_computation.13 | convolution fusion | flops 4297064448 | bytes 13631488 | tf_op jit(solution)/shard_map/phase_b/cond/branch_0_fun/dot_general | solution.py:80
  467.9 10.4 %conditional.20 = (bf16[512,1024]{1,0:T(8,128)(2,1)S(1)}, f32[512,4096]{1,0:T(8,128)}) conditional(s32[]{:T(128)} %convert_element_type.182, (bf16[512,1024]{1,0:T(8,128)(2,1)S(1)}, bf16[4096,1024]{1,0:T(8,128)(2,1)}) %tuple.155, (bf16[512,4096]{1,0:T(8,128)(2,1)}, bf16[4096,1024]{1,0:T(8,128)(2,1)}) %tuple.156), branch_computations={%region_20.21_spmd, %region_21.22_spmd} | conditional | flops 4299161600 | bytes 22020116 | solution.py:85
  480.6 20.4 %collective-permute-done.23 = bf16[512,4096]{1,0:T(8,128)(2,1)} collective-permute-done((bf16[512,4096]{1,0:T(8,128)(2,1)}, bf16[512,4096]{1,0:T(8,128)(2,1)}, u32[]{:S(2)}, u32[]{:S(2)}) %collective-permute-start.23) | collective-permute-done | bytes 4194336 | tf_op jit(solution)/shard_map/phase_b/ppermute | solution.py:66
  501.1 55.2 %collective-permute-done.24 = bf16[512,4096]{1,0:T(8,128)(2,1)} collective-permute-done((bf16[512,4096]{1,0:T(8,128)(2,1)}, bf16[512,4096]{1,0:T(8,128)(2,1)}, u32[]{:S(2)}, u32[]{:S(2)}) %collective-permute-start.24) | collective-permute-done | bytes 4194336 | tf_op jit(solution)/shard_map/phase_b/ppermute | solution.py:66
  572.1 18.0 %pmax.15 = f32[8,32]{0,1:T(8,128)S(1)} all-reduce(f32[8,32]{0,1:T(8,128)S(1)} %bitcast_reduce_fusion), channel_id=1, replica_groups=mesh['dp'=4,'section'=2,'tensor'=4] {'tensor'}, use_global_device_ids=true, to_apply=%region_24.25 | all-reduce | flops 256 | bytes 2048 | tf_op jit(solution)/shard_map/phase_b/pmax | solution.py:129
  590.4 23.9 %fusion.58 = (bf16[1,8,64,4096]{3,2,1,0:T(8,128)(2,1)}, bf16[1,8,64,4096]{3,2,1,0:T(8,128)(2,1)}) fusion(bf16[8,64,4096]{2,1,0:T(8,128)(2,1)} %copy-done.6, f32[8,64,4096]{2,1,0:T(8,128)} %copy-done, bf16[8,64,4096]{2,1,0:T(8,128)(2,1)} %copy-done.8, f32[8,64]{1,0:T(8,128)S(1)} %broadcast_multiply_fusion, f32[8,64]{1,0:T(8,128)S(1)} %copy-done.18, ...), kind=kLoop, calls=%fused_computation.106 | loop fusion | flops 144703488 | bytes 50991104 | tf_op jit(solution)/shard_map/broadcast_in_dim | solution.py:195
  614.3 25.2 %reduce-scatter.2.cloned.1.call-done = bf16[1024,1024]{1,0:T(8,128)(2,1)} async-done(((bf16[4096,1024]{1,0:T(8,128)(2,1)}), bf16[1024,1024]{1,0:T(8,128)(2,1)}) %reduce-scatter.2.cloned.1.call-update) | async-done | bytes 2097168 | tf_op jit(solution)/shard_map/weight_grad/reduce_scatter | solution.py:182
  (163 shorter events, 217.1 us)
Async XLA Ops:
  7.2 155.7 %all-gather.3.cloned.1.call-start = ((), (), s32[]{:S(2)}) async-start(), calls=%async_computation.2 | async-start | bytes 10485760 | tf_op jit(solution)/shard_map/all_gather | solution.py:71
  10.3 629.1 %reduce-scatter.2.cloned.1.call-start = ((), (), s32[]{:S(2)}) async-start(), calls=%async_computation.1 | async-start | bytes 10485760 | tf_op jit(solution)/shard_map/weight_grad/reduce_scatter | solution.py:182
  23.1 139.7 %collective-permute-start.1 = (bf16[512,4096]{1,0:T(8,128)(2,1)}, bf16[512,4096]{1,0:T(8,128)(2,1)}, u32[]{:S(2)}, u32[]{:S(2)}) collective-permute-start(bf16[512,4096]{1,0:T(8,128)(2,1)} %bitcast.5), channel_id=1, source_target_pairs={{0,8},{8,0},{16,24},{24,16},{1,9},{9,1},{17,25},{25,17},{2,10},{10... | collective-permute-start | bytes 12582920 | tf_op jit(solution)/shard_map/phase_a/ppermute | solution.py:59
  28.5 148.6 %collective-permute-start.4 = (bf16[512,4096]{1,0:T(8,128)(2,1)}, bf16[512,4096]{1,0:T(8,128)(2,1)}, u32[]{:S(2)}, u32[]{:S(2)}) collective-permute-start(bf16[512,4096]{1,0:T(8,128)(2,1)} %bitcast.5), channel_id=1, source_target_pairs={{0,16},{8,24},{16,0},{24,8},{1,17},{9,25},{17,1},{25,9},{2,18},{10... | collective-permute-start | bytes 12582920 | tf_op jit(solution)/shard_map/phase_a/ppermute | solution.py:59
  31.9 159.5 %collective-permute-start.7 = (bf16[512,4096]{1,0:T(8,128)(2,1)}, bf16[512,4096]{1,0:T(8,128)(2,1)}, u32[]{:S(2)}, u32[]{:S(2)}) collective-permute-start(bf16[512,4096]{1,0:T(8,128)(2,1)} %bitcast.5), channel_id=1, source_target_pairs={{0,24},{8,16},{16,8},{24,0},{1,25},{9,17},{17,9},{25,1},{2,26},{10... | collective-permute-start | bytes 12582920 | tf_op jit(solution)/shard_map/phase_a/ppermute | solution.py:59
  38.4 138.6 %collective-permute-start.3 = (bf16[512,1024]{1,0:T(8,128)(2,1)}, bf16[512,1024]{1,0:T(8,128)(2,1)}, u32[]{:S(2)}, u32[]{:S(2)}) collective-permute-start(bf16[512,1024]{1,0:T(8,128)(2,1)} %get-tuple-element.202), channel_id=1, source_target_pairs={{4,20},{12,28},{20,4},{28,12},{5,21},{13,29},{21,5},{29,13},{6,22}... | collective-permute-start | bytes 3145736 | tf_op jit(solution)/shard_map/phase_a/ppermute | solution.py:59
  41.1 150.3 %collective-permute-start.6 = (bf16[512,1024]{1,0:T(8,128)(2,1)S(1)}, bf16[512,1024]{1,0:T(8,128)(2,1)}, u32[]{:S(2)}, u32[]{:S(2)}) collective-permute-start(bf16[512,1024]{1,0:T(8,128)(2,1)S(1)} %get-tuple-element.201), channel_id=1, source_target_pairs={{4,28},{12,20},{20,12},{28,4},{5,29},{13,21},{21,13},{29,5},{6,30}... | collective-permute-start | bytes 3145736 | tf_op jit(solution)/shard_map/phase_a/ppermute | solution.py:59
  173.6 50.3 %collective-permute-start.2 = (bf16[512,1024]{1,0:T(8,128)(2,1)}, bf16[512,1024]{1,0:T(8,128)(2,1)}, u32[]{:S(2)}, u32[]{:S(2)}) collective-permute-start(bf16[512,1024]{1,0:T(8,128)(2,1)} %get-tuple-element.170), channel_id=1, source_target_pairs={{0,8},{8,0},{16,24},{24,16},{1,9},{9,1},{17,25},{25,17},{2,10},{10... | collective-permute-start | bytes 3145736 | tf_op jit(solution)/shard_map/phase_a/ppermute | solution.py:66
  188.0 40.8 %collective-permute-start.5 = (bf16[512,1024]{1,0:T(8,128)(2,1)}, bf16[512,1024]{1,0:T(8,128)(2,1)}, u32[]{:S(2)}, u32[]{:S(2)}) collective-permute-start(bf16[512,1024]{1,0:T(8,128)(2,1)} %get-tuple-element.171), channel_id=1, source_target_pairs={{0,16},{8,24},{16,0},{24,8},{1,17},{9,25},{17,1},{25,9},{2,18},{10... | collective-permute-start | bytes 3145736 | tf_op jit(solution)/shard_map/phase_a/ppermute | solution.py:66
  202.5 29.1 %collective-permute-start.8 = (bf16[512,1024]{1,0:T(8,128)(2,1)}, bf16[512,1024]{1,0:T(8,128)(2,1)}, u32[]{:S(2)}, u32[]{:S(2)}) collective-permute-start(bf16[512,1024]{1,0:T(8,128)(2,1)} %get-tuple-element.172), channel_id=1, source_target_pairs={{0,24},{8,16},{16,8},{24,0},{1,25},{9,17},{17,9},{25,1},{2,26},{10... | collective-permute-start | bytes 3145736 | tf_op jit(solution)/shard_map/phase_a/ppermute | solution.py:66
  205.1 66.5 %collective-permute-start.10 = (bf16[512,4096]{1,0:T(8,128)(2,1)}, bf16[512,4096]{1,0:T(8,128)(2,1)}, u32[]{:S(2)}, u32[]{:S(2)}) collective-permute-start(bf16[512,4096]{1,0:T(8,128)(2,1)} %copy-done.19), channel_id=1, source_target_pairs={{4,12},{12,4},{20,28},{28,20},{5,13},{13,5},{21,29},{29,21},{6,14}... | collective-permute-start | bytes 12582920 | tf_op jit(solution)/shard_map/phase_a/ppermute | solution.py:66
  207.7 63.9 %collective-permute-start.11 = (bf16[512,4096]{1,0:T(8,128)(2,1)}, bf16[512,4096]{1,0:T(8,128)(2,1)}, u32[]{:S(2)}, u32[]{:S(2)}) collective-permute-start(bf16[512,4096]{1,0:T(8,128)(2,1)} %copy-done.20), channel_id=1, source_target_pairs={{4,20},{12,28},{20,4},{28,12},{5,21},{13,29},{21,5},{29,13},{6,22}... | collective-permute-start | bytes 12582920 | tf_op jit(solution)/shard_map/phase_a/ppermute | solution.py:66
  223.9 47.6 %collective-permute-start.12 = (bf16[512,4096]{1,0:T(8,128)(2,1)}, bf16[512,4096]{1,0:T(8,128)(2,1)}, u32[]{:S(2)}, u32[]{:S(2)}) collective-permute-start(bf16[512,4096]{1,0:T(8,128)(2,1)} %copy-done.21), channel_id=1, source_target_pairs={{4,28},{12,20},{20,12},{28,4},{5,29},{13,21},{21,13},{29,5},{6,30}... | collective-permute-start | bytes 12582920 | tf_op jit(solution)/shard_map/phase_a/ppermute | solution.py:66
  301.4 43.9 %collective-permute-start.13 = (bf16[8,64,4096]{2,1,0:T(8,128)(2,1)S(1)}, bf16[8,64,4096]{2,1,0:T(8,128)(2,1)S(1)}, u32[]{:S(2)}, u32[]{:S(2)}) collective-permute-start(bf16[8,64,4096]{2,1,0:T(8,128)(2,1)S(1)} %fusion.37), channel_id=1, source_target_pairs={{4,0},{5,1},{6,2},{7,3},{12,8},{13,9},{14,10},{15,11},{20,16},{21,... | collective-permute-start | bytes 12582920 | tf_op jit(solution)/shard_map/phase_a/ppermute | solution.py:162
  302.7 51.1 %collective-permute-start.15 = (bf16[512,4096]{1,0:T(8,128)(2,1)}, bf16[512,4096]{1,0:T(8,128)(2,1)}, u32[]{:S(2)}, u32[]{:S(2)}) collective-permute-start(bf16[512,4096]{1,0:T(8,128)(2,1)} %bitcast.16), channel_id=1, source_target_pairs={{4,12},{12,4},{20,28},{28,20},{5,13},{13,5},{21,29},{29,21},{6,14}... | collective-permute-start | bytes 12582920 | tf_op jit(solution)/shard_map/phase_a/ppermute | solution.py:59
  305.4 51.7 %collective-permute-start.18 = (bf16[512,4096]{1,0:T(8,128)(2,1)}, bf16[512,4096]{1,0:T(8,128)(2,1)}, u32[]{:S(2)}, u32[]{:S(2)}) collective-permute-start(bf16[512,4096]{1,0:T(8,128)(2,1)} %bitcast.16), channel_id=1, source_target_pairs={{4,20},{12,28},{20,4},{28,12},{5,21},{13,29},{21,5},{29,13},{6,22}... | collective-permute-start | bytes 12582920 | tf_op jit(solution)/shard_map/phase_a/ppermute | solution.py:59
  308.0 49.1 %collective-permute-start.21 = (bf16[512,4096]{1,0:T(8,128)(2,1)}, bf16[512,4096]{1,0:T(8,128)(2,1)}, u32[]{:S(2)}, u32[]{:S(2)}) collective-permute-start(bf16[512,4096]{1,0:T(8,128)(2,1)} %bitcast.16), channel_id=1, source_target_pairs={{4,28},{12,20},{20,12},{28,4},{5,29},{13,21},{21,13},{29,5},{6,30}... | collective-permute-start | bytes 12582920 | tf_op jit(solution)/shard_map/phase_a/ppermute | solution.py:59
  347.8 28.0 %collective-permute-start.14 = (bf16[512,1024]{1,0:T(8,128)(2,1)S(1)}, bf16[512,1024]{1,0:T(8,128)(2,1)}, u32[]{:S(2)}, u32[]{:S(2)}) collective-permute-start(bf16[512,1024]{1,0:T(8,128)(2,1)S(1)} %get-tuple-element.196), channel_id=1, source_target_pairs={{0,8},{8,0},{16,24},{24,16},{1,9},{9,1},{17,25},{25,17},{2,10},{10... | collective-permute-start | bytes 3145736 | tf_op jit(solution)/shard_map/phase_a/ppermute | solution.py:59
  350.3 29.6 %collective-permute-start.17 = (bf16[512,1024]{1,0:T(8,128)(2,1)S(1)}, bf16[512,1024]{1,0:T(8,128)(2,1)}, u32[]{:S(2)}, u32[]{:S(2)}) collective-permute-start(bf16[512,1024]{1,0:T(8,128)(2,1)S(1)} %get-tuple-element.199), channel_id=1, source_target_pairs={{0,16},{8,24},{16,0},{24,8},{1,17},{9,25},{17,1},{25,9},{2,18},{10... | collective-permute-start | bytes 3145736 | tf_op jit(solution)/shard_map/phase_a/ppermute | solution.py:59
  353.7 45.5 %collective-permute-start.20 = (bf16[512,1024]{1,0:T(8,128)(2,1)S(1)}, bf16[512,1024]{1,0:T(8,128)(2,1)}, u32[]{:S(2)}, u32[]{:S(2)}) collective-permute-start(bf16[512,1024]{1,0:T(8,128)(2,1)S(1)} %get-tuple-element.198), channel_id=1, source_target_pairs={{0,24},{8,16},{16,8},{24,0},{1,25},{9,17},{17,9},{25,1},{2,26},{10... | collective-permute-start | bytes 3145736 | tf_op jit(solution)/shard_map/phase_a/ppermute | solution.py:59
  434.1 67.0 %collective-permute-start.23 = (bf16[512,4096]{1,0:T(8,128)(2,1)}, bf16[512,4096]{1,0:T(8,128)(2,1)}, u32[]{:S(2)}, u32[]{:S(2)}) collective-permute-start(bf16[512,4096]{1,0:T(8,128)(2,1)} %get-tuple-element.182), channel_id=1, source_target_pairs={{0,8},{8,0},{16,24},{24,16},{1,9},{9,1},{17,25},{25,17},{2,10},{10... | collective-permute-start | bytes 12582920 | tf_op jit(solution)/shard_map/phase_b/ppermute | solution.py:66
  447.2 109.1 %collective-permute-start.24 = (bf16[512,4096]{1,0:T(8,128)(2,1)}, bf16[512,4096]{1,0:T(8,128)(2,1)}, u32[]{:S(2)}, u32[]{:S(2)}) collective-permute-start(bf16[512,4096]{1,0:T(8,128)(2,1)} %get-tuple-element.183), channel_id=1, source_target_pairs={{0,16},{8,24},{16,0},{24,8},{1,17},{9,25},{17,1},{25,9},{2,18},{10... | collective-permute-start | bytes 12582920 | tf_op jit(solution)/shard_map/phase_b/ppermute | solution.py:66
  461.1 95.2 %collective-permute-start.25 = (bf16[512,4096]{1,0:T(8,128)(2,1)}, bf16[512,4096]{1,0:T(8,128)(2,1)}, u32[]{:S(2)}, u32[]{:S(2)}) collective-permute-start(bf16[512,4096]{1,0:T(8,128)(2,1)} %get-tuple-element.184), channel_id=1, source_target_pairs={{0,24},{8,16},{16,8},{24,0},{1,25},{9,17},{17,9},{25,1},{2,26},{10... | collective-permute-start | bytes 12582920 | tf_op jit(solution)/shard_map/phase_b/ppermute | solution.py:66
  466.1 14.0 %collective-permute-start.19 = (bf16[512,1024]{1,0:T(8,128)(2,1)}, bf16[512,1024]{1,0:T(8,128)(2,1)S(1)}, u32[]{:S(2)}, u32[]{:S(2)}) collective-permute-start(bf16[512,1024]{1,0:T(8,128)(2,1)} %copy-done.16), channel_id=1, source_target_pairs={{4,20},{12,28},{20,4},{28,12},{5,21},{13,29},{21,5},{29,13},{6,22}... | collective-permute-start | bytes 3145736 | tf_op jit(solution)/shard_map/phase_b/ppermute | solution.py:66
  (33 other events, 494.9 us)
Sparse Core Ops, SparseCore 0:
  10.4 152.3 all-gather.2
  423.4 216.0 reduce-scatter.1
where the time goes:
time: 660 us; the launch traced here: 651 us
  waiting for transfers between devices  299 us (45%)
  matrix products  104 us (16%)
  other arithmetic  101 us (15%)
  starting transfers between devices  65.6 us (10%)
  blocking collectives  33.9 us (5%)
  local copies, waits for them, and re-layouts  29.3 us (4%)
  between operations  15.3 us (2%)
    all_gather x1, waiting for transfers between devices, local(): lax.all_gather(columns(weight[0], replica), 'tensor', axis=0, tiled=True)  120 us
    ppermute x12, waiting for transfers between devices, give_back(): return lax.ppermute(value, ('dp', 'section'), pairs)  77.2 us
    ppermute x12, waiting for transfers between devices, exchange(): return lax.ppermute(value, ('dp', 'section'), pairs)  42.2 us
    dot_general x4, matrix products, backward(): lax.dot_general(piece, weight_part, (((1,), (1,)), ((), ())), preferred_e...  40.9 us
    dot_general x4, matrix products, forward(): out = jnp.dot(whole, weight_part, preferred_element_type=f32).astype(bf16)  39.7 us
    ppermute x1, waiting for transfers between devices, local(): upstream = lax.ppermute(grads[c], 'section', [(1, 0)])  34.6 us
    pmax x2, blocking collectives, finish_forward(): spread = lax.pmax(peak, 'tensor') + epsilon  33.9 us
    ppermute x12, starting transfers between devices, exchange(): return lax.ppermute(value, ('dp', 'section'), pairs)  32.1 us
  transfers between devices with their start and end apart: 28, of which 9 were waited for; matrix products, arithmetic and copies ran while one was open for 28% of the time, Pallas kernels for 0%

commit v1 on v0

--- a/solution.py
+++ b/solution.py
@@ -68,7 +68,12 @@
     def columns(value, index):
         return lax.dynamic_slice_in_dim(value, index * part, part, 1)
 
-    weight_part = lax.all_gather(columns(weight[0], replica), "tensor", axis=0, tiled=True)
+    weight_part = jnp.concatenate(
+        lax.all_to_all(
+            jnp.stack([columns(weight[0], replica)] * lax.axis_size("tensor")), "tensor", 0, 0
+        ),
+        axis=0,
+    )
 
     def product(forward_here, whole, piece):
 

time: 660 us -> 703 us (1.065)
  waiting for transfers between devices: 299 us -> 331 us
    all_to_all x0 -> x1, waiting for transfers between devices: none -> 154 us  [local(): lax.all_to_all(jnp.stack([columns(weight[0], replica)] * lax.axis_size('t...]
    all_gather x1 -> x0, waiting for transfers between devices: 120 us -> none  [local(): lax.all_gather(columns(weight[0], replica), 'tensor', axis=0, tiled=True)]
    another operation x10 -> x12, local copies, waits for them, and re-layouts: 8.33 us -> 16.5 us
  transfers between devices with their start and end apart: 28 -> 28, of which waited for: 9 -> 9; matrix products, arithmetic and copies ran while one was open for 28% -> 26% of each run, Pallas kernels for 0% -> 0%
where the time goes in v1:
time: 703 us; the launch traced here: 694 us
  waiting for transfers between devices  331 us (47%)
  matrix products  104 us (15%)
  other arithmetic  100 us (14%)
  starting transfers between devices  70.8 us (10%)
  blocking collectives  36 us (5%)
  local copies, waits for them, and re-layouts  34.4 us (5%)
  between operations  15.3 us (2%)
    all_to_all x1, waiting for transfers between devices, local(): lax.all_to_all(jnp.stack([columns(weight[0], replica)] * lax.axis_size('t...  154 us
    ppermute x12, waiting for transfers between devices, give_back(): return lax.ppermute(value, ('dp', 'section'), pairs)  77.3 us
    ppermute x12, waiting for transfers between devices, exchange(): return lax.ppermute(value, ('dp', 'section'), pairs)  42 us
    dot_general x4, matrix products, backward(): lax.dot_general(piece, weight_part, (((1,), (1,)), ((), ())), preferred_e...  40.9 us
    dot_general x4, matrix products, forward(): out = jnp.dot(whole, weight_part, preferred_element_type=f32).astype(bf16)  39.7 us
    pmax x2, blocking collectives, finish_forward(): spread = lax.pmax(peak, 'tensor') + epsilon  36 us
    ppermute x1, waiting for transfers between devices, local(): upstream = lax.ppermute(grads[c], 'section', [(1, 0)])  32.4 us
    ppermute x12, starting transfers between devices, exchange(): return lax.ppermute(value, ('dp', 'section'), pairs)  30.9 us
  transfers between devices with their start and end apart: 28, of which 9 were waited for; matrix products, arithmetic and copies ran while one was open for 26% of the time, Pallas kernels for 0%

profile of v1, /device:TPU:0, one launch (start us, length us, event | category | flops | bytes accessed | tf_op | source)
XLA Modules:
  0.0 694.1 jit_solution(12847464152657061611)
XLA Ops:
  49.9 154.0 %all-to-all-done = bf16[4,1024,1024]{2,1,0:T(8,128)(2,1)} async-done(((bf16[4,1024,1024]{2,1,0:T(8,128)(2,1)}), bf16[4,1024,1024]{2,1,0:T(8,128)(2,1)}, u32[]{:S(2)}, u32[]{:S(2)}) %all-to-all-start) | async-done | bytes 8388640 | tf_op jit(solution)/shard_map/all_to_all | solution.py:72
  203.9 10.8 %conditional.13 = (bf16[512,1024]{1,0:T(8,128)(2,1)}, bf16[512,4096]{1,0:T(8,128)(2,1)S(1)}) conditional(s32[]{:T(128)} %convert_element_type.174, (bf16[512,1024]{1,0:T(8,128)(2,1)}, bf16[4096,1024]{1,0:T(8,128)(2,1)}) %tuple.139, (bf16[512,4096]{1,0:T(8,128)(2,1)}, bf16[4096,1024]{1,0:T(8,128)(2,1)}) %tuple.86), branch_computations={%region_1.0_spmd, %region_2.0_spmd} | conditional | flops 4297064448 | bytes 17825810 | solution.py:90
  203.9 10.3 %convolution_convert_fusion.1 = bf16[512,1024]{1,0:T(8,128)(2,1)} fusion(bf16[512,4096]{1,0:T(8,128)(2,1)} %get-tuple-element.105, bf16[4096,1024]{1,0:T(8,128)(2,1)} %get-tuple-element.106), kind=kOutput, calls=%fused_computation.1 | convolution fusion | flops 4295491584 | bytes 13631488 | tf_op jit(solution)/shard_map/phase_a/cond/branch_1_fun/dot_general | solution.py:81
  218.2 10.9 %conditional.14 = (bf16[512,1024]{1,0:T(8,128)(2,1)}, bf16[512,4096]{1,0:T(8,128)(2,1)S(1)}) conditional(s32[]{:T(128)} %convert_element_type.174, (bf16[512,1024]{1,0:T(8,128)(2,1)}, bf16[4096,1024]{1,0:T(8,128)(2,1)}) %tuple.87, (bf16[512,4096]{1,0:T(8,128)(2,1)}, bf16[4096,1024]{1,0:T(8,128)(2,1)}) %tuple.88), branch_computations={%region_3.0_spmd, %region_4.0_spmd} | conditional | flops 4297064448 | bytes 17825810 | solution.py:90
  232.6 13.1 %conditional.15 = (bf16[512,1024]{1,0:T(8,128)(2,1)}, bf16[512,4096]{1,0:T(8,128)(2,1)}) conditional(s32[]{:T(128)} %convert_element_type.174, (bf16[512,1024]{1,0:T(8,128)(2,1)}, bf16[4096,1024]{1,0:T(8,128)(2,1)}) %tuple.89, (bf16[512,4096]{1,0:T(8,128)(2,1)}, bf16[4096,1024]{1,0:T(8,128)(2,1)}) %tuple.90), branch_computations={%region_5.0_spmd, %region_6.0_spmd} | conditional | flops 4297064448 | bytes 17825810 | solution.py:90
  253.5 13.5 %conditional.16 = (bf16[512,1024]{1,0:T(8,128)(2,1)S(1)}, f32[512,4096]{1,0:T(8,128)}) conditional(s32[]{:T(128)} %convert_element_type.174, (bf16[512,1024]{1,0:T(8,128)(2,1)S(1)}, bf16[4096,1024]{1,0:T(8,128)(2,1)}) %tuple.91, (bf16[512,4096]{1,0:T(8,128)(2,1)}, bf16[4096,1024]{1,0:T(8,128)(2,1)}) %tuple.92), branch_computations={%region_7.0_spmd, %region_8.0_spmd} | conditional | flops 4299161600 | bytes 22020116 | solution.py:90
  286.3 16.9 %pmax.14 = f32[8,32]{0,1:T(8,128)S(1)} all-reduce(f32[8,32]{0,1:T(8,128)S(1)} %bitcast_reduce_fusion.1), channel_id=1, replica_groups=mesh['dp'=4,'section'=2,'tensor'=4] {'tensor'}, use_global_device_ids=true, to_apply=%region_11.0 | all-reduce | flops 256 | bytes 2048 | tf_op jit(solution)/shard_map/phase_a/pmax | solution.py:134
  315.6 10.5 %add_convert_fusion.1 = bf16[512,4096]{1,0:T(8,128)(2,1)} fusion(f32[512,4096]{1,0:T(8,128)} %get-tuple-element.177, bf16[512,4096]{1,0:T(8,128)(2,1)} %collective-permute-done.12, bf16[512,4096]{1,0:T(8,128)(2,1)} %collective-permute-done.11, bf16[512,4096]{1,0:T(8,128)(2,1)} %collective-permute-done.10), kind=kLoop, calls=%fused_computation.86 | loop fusion | flops 14680064 | bytes 25165824 | tf_op jit(solution)/shard_map/phase_a/convert_element_type | solution.py:143
  354.8 32.4 %collective-permute-done.13 = bf16[8,64,4096]{2,1,0:T(8,128)(2,1)S(1)} collective-permute-done((bf16[8,64,4096]{2,1,0:T(8,128)(2,1)S(1)}, bf16[8,64,4096]{2,1,0:T(8,128)(2,1)S(1)}, u32[]{:S(2)}, u32[]{:S(2)}) %collective-permute-start.13) | collective-permute-done | bytes 4194336 | tf_op jit(solution)/shard_map/phase_a/ppermute | solution.py:167
  399.0 18.8 %collective-permute-done.14 = bf16[512,1024]{1,0:T(8,128)(2,1)} collective-permute-done((bf16[512,1024]{1,0:T(8,128)(2,1)S(1)}, bf16[512,1024]{1,0:T(8,128)(2,1)}, u32[]{:S(2)}, u32[]{:S(2)}) %collective-permute-start.14) | collective-permute-done | bytes 1048608 | tf_op jit(solution)/shard_map/phase_a/ppermute | solution.py:59
  423.3 17.6 %collective-permute-done.20 = bf16[512,1024]{1,0:T(8,128)(2,1)} collective-permute-done((bf16[512,1024]{1,0:T(8,128)(2,1)S(1)}, bf16[512,1024]{1,0:T(8,128)(2,1)}, u32[]{:S(2)}, u32[]{:S(2)}) %collective-permute-start.20) | collective-permute-done | bytes 1048608 | tf_op jit(solution)/shard_map/phase_a/ppermute | solution.py:59
  440.9 24.0 %conditional.21 = (bf16[4096,1024]{1,0:T(8,128)(2,1)}) conditional(s32[]{:T(128)} %convert_element_type.174, (bf16[512,4096]{1,0:T(8,128)(2,1)}, bf16[512,4096]{1,0:T(8,128)(2,1)}, bf16[512,4096]{1,0:T(8,128)(2,1)}, bf16[512,4096]{1,0:T(8,128)(2,1)}, bf16[512,1024]{1,0:T(8,128)(2,1)S(1)}, /*index=5*/bf16[512,1024]{1,0:T(8,128)(2,1)}, ...), branch_computations={%region_26.27_spmd, %region_27.28_spmd} | conditional | flops 17263755264 | bytes 29360136
  441.1 23.8 %fusion.18 = bf16[4096,1024]{1,0:T(8,128)(2,1)} fusion(bf16[512,4096]{1,0:T(8,128)(2,1)} %get-tuple-element.146, bf16[512,4096]{1,0:T(8,128)(2,1)} %get-tuple-element.145, bf16[512,4096]{1,0:T(8,128)(2,1)} %get-tuple-element.144, bf16[512,4096]{1,0:T(8,128)(2,1)} %get-tuple-element.143, bf16[512,1024]{1,0:T(8,128)(2,1)} %get-tuple-element.150, ...), kind=kOutput, calls=%fused_computation.34 | convolution fusion | flops 17263755264 | bytes 29360128 | tf_op jit(solution)/shard_map/weight_grad/cond/branch_1_fun/dot_general | solution.py:174
  465.0 10.8 %conditional.17 = (bf16[512,1024]{1,0:T(8,128)(2,1)S(1)}, bf16[512,4096]{1,0:T(8,128)(2,1)}) conditional(s32[]{:T(128)} %convert_element_type.182, (bf16[512,1024]{1,0:T(8,128)(2,1)}, bf16[4096,1024]{1,0:T(8,128)(2,1)}) %tuple.93, (bf16[512,4096]{1,0:T(8,128)(2,1)}, bf16[4096,1024]{1,0:T(8,128)(2,1)}) %tuple.94), branch_computations={%region_14.15_spmd, %region_15.16_spmd} | conditional | flops 4297064448 | bytes 17825810 | solution.py:90
  479.2 10.6 %conditional.18 = (bf16[512,1024]{1,0:T(8,128)(2,1)S(1)}, bf16[512,4096]{1,0:T(8,128)(2,1)}) conditional(s32[]{:T(128)} %convert_element_type.182, (bf16[512,1024]{1,0:T(8,128)(2,1)}, bf16[4096,1024]{1,0:T(8,128)(2,1)}) %tuple.95, (bf16[512,4096]{1,0:T(8,128)(2,1)}, bf16[4096,1024]{1,0:T(8,128)(2,1)}) %tuple.96), branch_computations={%region_16.17_spmd, %region_17.18_spmd} | conditional | flops 4297064448 | bytes 17825810 | solution.py:90
  479.2 10.3 %convolution_convert_fusion.10 = bf16[512,4096]{1,0:T(8,128)(2,1)} fusion(bf16[512,1024]{1,0:T(8,128)(2,1)} %get-tuple-element.123, bf16[4096,1024]{1,0:T(8,128)(2,1)} %get-tuple-element.124), kind=kOutput, calls=%fused_computation.11 | convolution fusion | flops 4297064448 | bytes 13631488 | tf_op jit(solution)/shard_map/phase_b/cond/branch_0_fun/dot_general | solution.py:85
  492.2 11.4 %conditional.19 = (bf16[512,1024]{1,0:T(8,128)(2,1)}, bf16[512,4096]{1,0:T(8,128)(2,1)}) conditional(s32[]{:T(128)} %convert_element_type.182, (bf16[512,1024]{1,0:T(8,128)(2,1)}, bf16[4096,1024]{1,0:T(8,128)(2,1)}) %tuple.97, (bf16[512,4096]{1,0:T(8,128)(2,1)}, bf16[4096,1024]{1,0:T(8,128)(2,1)}) %tuple.98), branch_computations={%region_18.19_spmd, %region_19.20_spmd} | conditional | flops 4297064448 | bytes 17825810 | solution.py:90
  492.2 10.3 %convolution_convert_fusion.12 = bf16[512,4096]{1,0:T(8,128)(2,1)} fusion(bf16[512,1024]{1,0:T(8,128)(2,1)} %get-tuple-element.127, bf16[4096,1024]{1,0:T(8,128)(2,1)} %get-tuple-element.128), kind=kOutput, calls=%fused_computation.13 | convolution fusion | flops 4297064448 | bytes 13631488 | tf_op jit(solution)/shard_map/phase_b/cond/branch_0_fun/dot_general | solution.py:85
  509.5 10.4 %conditional.20 = (bf16[512,1024]{1,0:T(8,128)(2,1)S(1)}, f32[512,4096]{1,0:T(8,128)}) conditional(s32[]{:T(128)} %convert_element_type.182, (bf16[512,1024]{1,0:T(8,128)(2,1)S(1)}, bf16[4096,1024]{1,0:T(8,128)(2,1)}) %tuple.99, (bf16[512,4096]{1,0:T(8,128)(2,1)}, bf16[4096,1024]{1,0:T(8,128)(2,1)}) %tuple.100), branch_computations={%region_20.21_spmd, %region_21.22_spmd} | conditional | flops 4299161600 | bytes 22020116 | solution.py:90
  522.3 20.6 %collective-permute-done.23 = bf16[512,4096]{1,0:T(8,128)(2,1)} collective-permute-done((bf16[512,4096]{1,0:T(8,128)(2,1)}, bf16[512,4096]{1,0:T(8,128)(2,1)}, u32[]{:S(2)}, u32[]{:S(2)}) %collective-permute-start.23) | collective-permute-done | bytes 4194336 | tf_op jit(solution)/shard_map/phase_b/ppermute | solution.py:66
  542.9 55.0 %collective-permute-done.24 = bf16[512,4096]{1,0:T(8,128)(2,1)} collective-permute-done((bf16[512,4096]{1,0:T(8,128)(2,1)}, bf16[512,4096]{1,0:T(8,128)(2,1)}, u32[]{:S(2)}, u32[]{:S(2)}) %collective-permute-start.24) | collective-permute-done | bytes 4194336 | tf_op jit(solution)/shard_map/phase_b/ppermute | solution.py:66
  613.8 19.1 %pmax.15 = f32[8,32]{0,1:T(8,128)S(1)} all-reduce(f32[8,32]{0,1:T(8,128)S(1)} %bitcast_reduce_fusion), channel_id=1, replica_groups=mesh['dp'=4,'section'=2,'tensor'=4] {'tensor'}, use_global_device_ids=true, to_apply=%region_24.25 | all-reduce | flops 256 | bytes 2048 | tf_op jit(solution)/shard_map/phase_b/pmax | solution.py:134
  633.2 24.0 %fusion.58 = (bf16[1,8,64,4096]{3,2,1,0:T(8,128)(2,1)}, bf16[1,8,64,4096]{3,2,1,0:T(8,128)(2,1)}) fusion(bf16[8,64,4096]{2,1,0:T(8,128)(2,1)} %copy-done.6, f32[8,64,4096]{2,1,0:T(8,128)} %copy-done, bf16[8,64,4096]{2,1,0:T(8,128)(2,1)} %copy-done.8, f32[8,64]{1,0:T(8,128)S(1)} %broadcast_multiply_fusion, f32[8,64]{1,0:T(8,128)S(1)} %copy-done.18, ...), kind=kLoop, calls=%fused_computation.106 | loop fusion | flops 144703488 | bytes 50991104 | tf_op jit(solution)/shard_map/broadcast_in_dim | solution.py:200
  657.2 25.6 %reduce-scatter.2.cloned.1.call-done = bf16[1024,1024]{1,0:T(8,128)(2,1)} async-done(((bf16[4096,1024]{1,0:T(8,128)(2,1)}), bf16[1024,1024]{1,0:T(8,128)(2,1)}) %reduce-scatter.2.cloned.1.call-update) | async-done | bytes 2097168 | tf_op jit(solution)/shard_map/weight_grad/reduce_scatter | solution.py:187
  (163 shorter events, 228.0 us)
Async XLA Ops:
  13.3 190.6 %all-to-all-start = ((bf16[4,1024,1024]{2,1,0:T(8,128)(2,1)}), bf16[4,1024,1024]{2,1,0:T(8,128)(2,1)}, u32[]{:S(2)}, u32[]{:S(2)}) async-start(bf16[4,1024,1024]{2,1,0:T(8,128)(2,1)} %stack.10), calls=%async_computation | async-start | bytes 16777216 | tf_op jit(solution)/shard_map/all_to_all | solution.py:72
  19.8 663.0 %reduce-scatter.2.cloned.1.call-start = ((), (), s32[]{:S(2)}) async-start(), calls=%async_computation.2 | async-start | bytes 10485760 | tf_op jit(solution)/shard_map/weight_grad/reduce_scatter | solution.py:187
  31.5 172.5 %collective-permute-start.1 = (bf16[512,4096]{1,0:T(8,128)(2,1)}, bf16[512,4096]{1,0:T(8,128)(2,1)}, u32[]{:S(2)}, u32[]{:S(2)}) collective-permute-start(bf16[512,4096]{1,0:T(8,128)(2,1)} %bitcast.6), channel_id=1, source_target_pairs={{0,8},{8,0},{16,24},{24,16},{1,9},{9,1},{17,25},{25,17},{2,10},{10... | collective-permute-start | bytes 12582920 | tf_op jit(solution)/shard_map/phase_a/ppermute | solution.py:59
  35.7 182.5 %collective-permute-start.4 = (bf16[512,4096]{1,0:T(8,128)(2,1)}, bf16[512,4096]{1,0:T(8,128)(2,1)}, u32[]{:S(2)}, u32[]{:S(2)}) collective-permute-start(bf16[512,4096]{1,0:T(8,128)(2,1)} %bitcast.6), channel_id=1, source_target_pairs={{0,16},{8,24},{16,0},{24,8},{1,17},{9,25},{17,1},{25,9},{2,18},{10... | collective-permute-start | bytes 12582920 | tf_op jit(solution)/shard_map/phase_a/ppermute | solution.py:59
  39.1 193.5 %collective-permute-start.7 = (bf16[512,4096]{1,0:T(8,128)(2,1)}, bf16[512,4096]{1,0:T(8,128)(2,1)}, u32[]{:S(2)}, u32[]{:S(2)}) collective-permute-start(bf16[512,4096]{1,0:T(8,128)(2,1)} %bitcast.6), channel_id=1, source_target_pairs={{0,24},{8,16},{16,8},{24,0},{1,25},{9,17},{17,9},{25,1},{2,26},{10... | collective-permute-start | bytes 12582920 | tf_op jit(solution)/shard_map/phase_a/ppermute | solution.py:59
  45.6 172.6 %collective-permute-start.3 = (bf16[512,1024]{1,0:T(8,128)(2,1)}, bf16[512,1024]{1,0:T(8,128)(2,1)}, u32[]{:S(2)}, u32[]{:S(2)}) collective-permute-start(bf16[512,1024]{1,0:T(8,128)(2,1)} %get-tuple-element.202), channel_id=1, source_target_pairs={{4,20},{12,28},{20,4},{28,12},{5,21},{13,29},{21,5},{29,13},{6,22}... | collective-permute-start | bytes 3145736 | tf_op jit(solution)/shard_map/phase_a/ppermute | solution.py:59
  48.3 184.3 %collective-permute-start.6 = (bf16[512,1024]{1,0:T(8,128)(2,1)S(1)}, bf16[512,1024]{1,0:T(8,128)(2,1)}, u32[]{:S(2)}, u32[]{:S(2)}) collective-permute-start(bf16[512,1024]{1,0:T(8,128)(2,1)S(1)} %get-tuple-element.201), channel_id=1, source_target_pairs={{4,28},{12,20},{20,12},{28,4},{5,29},{13,21},{21,13},{29,5},{6,30}... | collective-permute-start | bytes 3145736 | tf_op jit(solution)/shard_map/phase_a/ppermute | solution.py:59
  214.7 52.3 %collective-permute-start.2 = (bf16[512,1024]{1,0:T(8,128)(2,1)}, bf16[512,1024]{1,0:T(8,128)(2,1)}, u32[]{:S(2)}, u32[]{:S(2)}) collective-permute-start(bf16[512,1024]{1,0:T(8,128)(2,1)} %get-tuple-element.170), channel_id=1, source_target_pairs={{0,8},{8,0},{16,24},{24,16},{1,9},{9,1},{17,25},{25,17},{2,10},{10... | collective-permute-start | bytes 3145736 | tf_op jit(solution)/shard_map/phase_a/ppermute | solution.py:66
  229.1 42.8 %collective-permute-start.5 = (bf16[512,1024]{1,0:T(8,128)(2,1)}, bf16[512,1024]{1,0:T(8,128)(2,1)}, u32[]{:S(2)}, u32[]{:S(2)}) collective-permute-start(bf16[512,1024]{1,0:T(8,128)(2,1)} %get-tuple-element.171), channel_id=1, source_target_pairs={{0,16},{8,24},{16,0},{24,8},{1,17},{9,25},{17,1},{25,9},{2,18},{10... | collective-permute-start | bytes 3145736 | tf_op jit(solution)/shard_map/phase_a/ppermute | solution.py:66
  245.7 29.2 %collective-permute-start.8 = (bf16[512,1024]{1,0:T(8,128)(2,1)}, bf16[512,1024]{1,0:T(8,128)(2,1)}, u32[]{:S(2)}, u32[]{:S(2)}) collective-permute-start(bf16[512,1024]{1,0:T(8,128)(2,1)} %get-tuple-element.172), channel_id=1, source_target_pairs={{0,24},{8,16},{16,8},{24,0},{1,25},{9,17},{17,9},{25,1},{2,26},{10... | collective-permute-start | bytes 3145736 | tf_op jit(solution)/shard_map/phase_a/ppermute | solution.py:66
  248.2 67.4 %collective-permute-start.11 = (bf16[512,4096]{1,0:T(8,128)(2,1)}, bf16[512,4096]{1,0:T(8,128)(2,1)}, u32[]{:S(2)}, u32[]{:S(2)}) collective-permute-start(bf16[512,4096]{1,0:T(8,128)(2,1)} %copy-done.21), channel_id=1, source_target_pairs={{4,20},{12,28},{20,4},{28,12},{5,21},{13,29},{21,5},{29,13},{6,22}... | collective-permute-start | bytes 12582920 | tf_op jit(solution)/shard_map/phase_a/ppermute | solution.py:66
  250.8 64.8 %collective-permute-start.12 = (bf16[512,4096]{1,0:T(8,128)(2,1)}, bf16[512,4096]{1,0:T(8,128)(2,1)}, u32[]{:S(2)}, u32[]{:S(2)}) collective-permute-start(bf16[512,4096]{1,0:T(8,128)(2,1)} %get-tuple-element.176), channel_id=1, source_target_pairs={{4,28},{12,20},{20,12},{28,4},{5,29},{13,21},{21,13},{29,5},{6,30}... | collective-permute-start | bytes 12582920 | tf_op jit(solution)/shard_map/phase_a/ppermute | solution.py:66
  267.0 48.6 %collective-permute-start.10 = (bf16[512,4096]{1,0:T(8,128)(2,1)}, bf16[512,4096]{1,0:T(8,128)(2,1)}, u32[]{:S(2)}, u32[]{:S(2)}) collective-permute-start(bf16[512,4096]{1,0:T(8,128)(2,1)} %copy-done.20), channel_id=1, source_target_pairs={{4,12},{12,4},{20,28},{28,20},{5,13},{13,5},{21,29},{29,21},{6,14}... | collective-permute-start | bytes 12582920 | tf_op jit(solution)/shard_map/phase_a/ppermute | solution.py:66
  345.5 41.7 %collective-permute-start.13 = (bf16[8,64,4096]{2,1,0:T(8,128)(2,1)S(1)}, bf16[8,64,4096]{2,1,0:T(8,128)(2,1)S(1)}, u32[]{:S(2)}, u32[]{:S(2)}) collective-permute-start(bf16[8,64,4096]{2,1,0:T(8,128)(2,1)S(1)} %fusion.37), channel_id=1, source_target_pairs={{4,0},{5,1},{6,2},{7,3},{12,8},{13,9},{14,10},{15,11},{20,16},{21,... | collective-permute-start | bytes 12582920 | tf_op jit(solution)/shard_map/phase_a/ppermute | solution.py:167
  346.7 49.6 %collective-permute-start.15 = (bf16[512,4096]{1,0:T(8,128)(2,1)}, bf16[512,4096]{1,0:T(8,128)(2,1)}, u32[]{:S(2)}, u32[]{:S(2)}) collective-permute-start(bf16[512,4096]{1,0:T(8,128)(2,1)} %bitcast.17), channel_id=1, source_target_pairs={{4,12},{12,4},{20,28},{28,20},{5,13},{13,5},{21,29},{29,21},{6,14}... | collective-permute-start | bytes 12582920 | tf_op jit(solution)/shard_map/phase_a/ppermute | solution.py:59
  349.5 49.5 %collective-permute-start.18 = (bf16[512,4096]{1,0:T(8,128)(2,1)}, bf16[512,4096]{1,0:T(8,128)(2,1)}, u32[]{:S(2)}, u32[]{:S(2)}) collective-permute-start(bf16[512,4096]{1,0:T(8,128)(2,1)} %bitcast.17), channel_id=1, source_target_pairs={{4,20},{12,28},{20,4},{28,12},{5,21},{13,29},{21,5},{29,13},{6,22}... | collective-permute-start | bytes 12582920 | tf_op jit(solution)/shard_map/phase_a/ppermute | solution.py:59
  352.1 46.9 %collective-permute-start.21 = (bf16[512,4096]{1,0:T(8,128)(2,1)}, bf16[512,4096]{1,0:T(8,128)(2,1)}, u32[]{:S(2)}, u32[]{:S(2)}) collective-permute-start(bf16[512,4096]{1,0:T(8,128)(2,1)} %bitcast.17), channel_id=1, source_target_pairs={{4,28},{12,20},{20,12},{28,4},{5,29},{13,21},{21,13},{29,5},{6,30}... | collective-permute-start | bytes 12582920 | tf_op jit(solution)/shard_map/phase_a/ppermute | solution.py:59
  389.7 28.0 %collective-permute-start.14 = (bf16[512,1024]{1,0:T(8,128)(2,1)S(1)}, bf16[512,1024]{1,0:T(8,128)(2,1)}, u32[]{:S(2)}, u32[]{:S(2)}) collective-permute-start(bf16[512,1024]{1,0:T(8,128)(2,1)S(1)} %get-tuple-element.196), channel_id=1, source_target_pairs={{0,8},{8,0},{16,24},{24,16},{1,9},{9,1},{17,25},{25,17},{2,10},{10... | collective-permute-start | bytes 3145736 | tf_op jit(solution)/shard_map/phase_a/ppermute | solution.py:59
  392.9 30.5 %collective-permute-start.17 = (bf16[512,1024]{1,0:T(8,128)(2,1)S(1)}, bf16[512,1024]{1,0:T(8,128)(2,1)}, u32[]{:S(2)}, u32[]{:S(2)}) collective-permute-start(bf16[512,1024]{1,0:T(8,128)(2,1)S(1)} %get-tuple-element.199), channel_id=1, source_target_pairs={{0,16},{8,24},{16,0},{24,8},{1,17},{9,25},{17,1},{25,9},{2,18},{10... | collective-permute-start | bytes 3145736 | tf_op jit(solution)/shard_map/phase_a/ppermute | solution.py:59
  396.3 44.6 %collective-permute-start.20 = (bf16[512,1024]{1,0:T(8,128)(2,1)S(1)}, bf16[512,1024]{1,0:T(8,128)(2,1)}, u32[]{:S(2)}, u32[]{:S(2)}) collective-permute-start(bf16[512,1024]{1,0:T(8,128)(2,1)S(1)} %get-tuple-element.198), channel_id=1, source_target_pairs={{0,24},{8,16},{16,8},{24,0},{1,25},{9,17},{17,9},{25,1},{2,26},{10... | collective-permute-start | bytes 3145736 | tf_op jit(solution)/shard_map/phase_a/ppermute | solution.py:59
  475.8 67.2 %collective-permute-start.23 = (bf16[512,4096]{1,0:T(8,128)(2,1)}, bf16[512,4096]{1,0:T(8,128)(2,1)}, u32[]{:S(2)}, u32[]{:S(2)}) collective-permute-start(bf16[512,4096]{1,0:T(8,128)(2,1)} %get-tuple-element.182), channel_id=1, source_target_pairs={{0,8},{8,0},{16,24},{24,16},{1,9},{9,1},{17,25},{25,17},{2,10},{10... | collective-permute-start | bytes 12582920 | tf_op jit(solution)/shard_map/phase_b/ppermute | solution.py:66
  489.8 108.1 %collective-permute-start.24 = (bf16[512,4096]{1,0:T(8,128)(2,1)}, bf16[512,4096]{1,0:T(8,128)(2,1)}, u32[]{:S(2)}, u32[]{:S(2)}) collective-permute-start(bf16[512,4096]{1,0:T(8,128)(2,1)} %get-tuple-element.183), channel_id=1, source_target_pairs={{0,16},{8,24},{16,0},{24,8},{1,17},{9,25},{17,1},{25,9},{2,18},{10... | collective-permute-start | bytes 12582920 | tf_op jit(solution)/shard_map/phase_b/ppermute | solution.py:66
  503.7 94.2 %collective-permute-start.25 = (bf16[512,4096]{1,0:T(8,128)(2,1)}, bf16[512,4096]{1,0:T(8,128)(2,1)}, u32[]{:S(2)}, u32[]{:S(2)}) collective-permute-start(bf16[512,4096]{1,0:T(8,128)(2,1)} %get-tuple-element.184), channel_id=1, source_target_pairs={{0,24},{8,16},{16,8},{24,0},{1,25},{9,17},{17,9},{25,1},{2,26},{10... | collective-permute-start | bytes 12582920 | tf_op jit(solution)/shard_map/phase_b/ppermute | solution.py:66
  507.8 14.0 %collective-permute-start.19 = (bf16[512,1024]{1,0:T(8,128)(2,1)}, bf16[512,1024]{1,0:T(8,128)(2,1)S(1)}, u32[]{:S(2)}, u32[]{:S(2)}) collective-permute-start(bf16[512,1024]{1,0:T(8,128)(2,1)} %copy-done.16), channel_id=1, source_target_pairs={{4,20},{12,28},{20,4},{28,12},{5,21},{13,29},{21,5},{29,13},{6,22}... | collective-permute-start | bytes 3145736 | tf_op jit(solution)/shard_map/phase_b/ppermute | solution.py:66
  (33 other events, 496.4 us)
Sparse Core Ops, SparseCore 0:
  465.1 217.6 reduce-scatter.1
